TPU v7x, 32 devices: a whole 2x2x4 slice. The times are simulated.
32 devices in a mesh: dp: 8 (over z, y), tensor: 4 (over x, core).
Axes of the slice: x: 2, y: 2, z: 4, core: 2. Of those that a mesh axis runs over, the one named last changes fastest.
Arguments:
- tokens: bfloat16 [3, 4096, 1536], P(None, ('dp', 'tensor')), may hold values from -6 to 6
- lengths: int32 [3, 32, 6], P(None, ('dp', 'tensor')), may hold values from 1 to 64, 128 in all within a row
- first_gain: bfloat16 [1536], P(('dp', 'tensor')), may hold values from 0.099609375 to 1.8984375
- query_weight: bfloat16 [1536, 1536], P(('dp', 'tensor')), may hold values from -0.15625 to 0.15625
- key_weight: bfloat16 [1536, 768], P(('dp', 'tensor')), may hold values from -0.15625 to 0.15625
- value_weight: bfloat16 [1536, 768], P(('dp', 'tensor')), may hold values from -0.15625 to 0.15625
- output_weight: bfloat16 [1536, 1536], P(('dp', 'tensor')), may hold values from -0.4375 to 0.4375
- second_gain: bfloat16 [1536], P(('dp', 'tensor')), may hold values from 0.099609375 to 1.8984375
- gate_weight: bfloat16 [1536, 4096], P('dp', 'tensor'), may hold values from -0.15625 to 0.15625
- up_weight: bfloat16 [1536, 4096], P('dp', 'tensor'), may hold values from -0.15625 to 0.15625
- down_weight: bfloat16 [4096, 1536], P('tensor', 'dp'), may hold values from -0.09375 to 0.09375
- cotangent: bfloat16 [3, 4096, 1536], P(None, ('dp', 'tensor')), may hold values from -6 to 6
Outputs:
- layer_out: bfloat16 [3, 4096, 1536], P(None, ('dp', 'tensor'))
- input_grad: float32 [3, 4096, 1536], P(None, ('dp', 'tensor'))
- first_gain_grad: float32 [1536], P(('dp', 'tensor'))
- query_grad: float32 [1536, 1536], P(('dp', 'tensor'))
- key_grad: float32 [1536, 768], P(('dp', 'tensor'))
- value_grad: float32 [1536, 768], P(('dp', 'tensor'))
- output_grad: float32 [1536, 1536], P(('dp', 'tensor'))
- second_gain_grad: float32 [1536], P(('dp', 'tensor'))
- gate_grad: float32 [1536, 4096], P('dp', 'tensor')
- up_grad: float32 [1536, 4096], P('dp', 'tensor')
- down_grad: float32 [4096, 1536], P('tensor', 'dp')
Inputs may be any that keep to these rules, and one draw needn't show every extreme that they name: Row lengths[m, p] splits the 128 rows of pack p of micro-batch m into 6 runs in order, summing to 128; the first 5 runs are sequences, the last is padding; no run is longer than 64 rows.
All inputs are finite; a program needn't handle non-finite values.
Results may differ from a plain program's by a relative error of at most 0.013.
Values may be sent and summed in bfloat16 or wider, within the bound.
No kernel may reach another device: no remote copies, remote signals or barrier semaphores. Data moves between devices by JAX's collectives and lax.ppermute only.
A program may use at most 192 MiB of HBM per device.

v0:
```python
import math
import jax
import jax.numpy as jnp
from jax import lax
from jax.sharding import PartitionSpec as P

HEADS = 16
KV_HEADS = 8
HEAD = 96
SLOTS = 6
EPSILON = 1e-05
ROPE_BASE = 100000.0
NEG_LARGE = -1e30


def pack_layout(seq_lengths, row_count):
    seq_ends = jnp.cumsum(seq_lengths)
    seq_starts = seq_ends - seq_lengths
    row_index = jnp.arange(row_count, dtype=jnp.int32)
    segment = jnp.sum((row_index[:, None] >= seq_ends[None, :]).astype(jnp.int32), axis=1)
    owner_hot = segment[:, None] == jnp.arange(seq_lengths.shape[0], dtype=jnp.int32)[None, :]
    position = row_index - jnp.sum(jnp.where(owner_hot, seq_starts[None, :], 0), axis=1)
    return (segment, position)


def rotary_tables(position, head_size):
    half_size = head_size // 2
    freq_index = jnp.arange(half_size, dtype=jnp.float32)
    inverse = jnp.exp(freq_index * (-2.0 / head_size) * math.log(ROPE_BASE))
    angles = position.astype(jnp.float32)[:, None] * inverse[None, :]
    return (jnp.cos(angles), jnp.sin(angles))


def rotate(vectors, cosine, sine_part):
    half_size = vectors.shape[-1] // 2
    lower_half = vectors[..., :half_size]
    upper_half = vectors[..., half_size:]
    cosine = cosine[:, None, :]
    sine_part = sine_part[:, None, :]
    return jnp.concatenate(
        [
            lower_half * cosine - upper_half * sine_part,
            upper_half * cosine + lower_half * sine_part,
        ],
        axis=-1,
    )


def unrotate(vectors, cosine, sine_part):
    half_size = vectors.shape[-1] // 2
    lower_half = vectors[..., :half_size]
    upper_half = vectors[..., half_size:]
    cosine = cosine[:, None, :]
    sine_part = sine_part[:, None, :]
    return jnp.concatenate(
        [
            lower_half * cosine + upper_half * sine_part,
            upper_half * cosine - lower_half * sine_part,
        ],
        axis=-1,
    )


def visible(segment, row_valid):
    row_index = jnp.arange(segment.shape[0], dtype=jnp.int32)
    same_seq = segment[:, None] == segment[None, :]
    return same_seq & (row_index[None, :] <= row_index[:, None]) & row_valid[:, None]


def product(left_side, right_side):
    return jnp.dot(left_side, right_side, preferred_element_type=jnp.float32)


def across(left_side, right_side):
    return lax.dot_general(
        left_side, right_side, (((0,), (0,)), ((), ())), preferred_element_type=jnp.float32
    )


def against(left_side, right_side):
    return lax.dot_general(
        left_side, right_side, (((1,), (1,)), ((), ())), preferred_element_type=jnp.float32
    )


def norm_back(upstream, signal, inverse, gain_vec):
    weighted = upstream * gain_vec
    gain_part = jnp.sum(upstream * signal * inverse, axis=0)
    signal_part = inverse * weighted - signal * (inverse * inverse * inverse) * jnp.mean(
        weighted * signal, axis=1, keepdims=True
    )
    return (signal_part, gain_part)


def fetch_attention(first_gain, query_weight, key_weight, value_weight, output_weight, second_gain):
    return (
        lax.all_gather(first_gain, ("dp", "tensor"), axis=0, tiled=True),
        lax.all_gather(query_weight, ("dp", "tensor"), axis=0, tiled=True),
        lax.all_gather(key_weight, ("dp", "tensor"), axis=0, tiled=True),
        lax.all_gather(value_weight, ("dp", "tensor"), axis=0, tiled=True),
        lax.all_gather(output_weight, ("dp", "tensor"), axis=0, tiled=True),
        lax.all_gather(second_gain, ("dp", "tensor"), axis=0, tiled=True),
    )


def fetch_mlp(gate_weight, up_weight, down_weight):
    return (
        lax.all_gather(gate_weight, "dp", axis=0, tiled=True),
        lax.all_gather(up_weight, "dp", axis=0, tiled=True),
        lax.all_gather(down_weight, "dp", axis=1, tiled=True),
    )


def reduce_attention(new_parts):
    return (
        lax.psum_scatter(new_parts[0], ("dp", "tensor"), scatter_dimension=0, tiled=True),
        lax.psum_scatter(new_parts[1], ("dp", "tensor"), scatter_dimension=0, tiled=True),
        lax.psum_scatter(new_parts[2], ("dp", "tensor"), scatter_dimension=0, tiled=True),
        lax.psum_scatter(new_parts[3], ("dp", "tensor"), scatter_dimension=0, tiled=True),
        lax.psum_scatter(new_parts[4], ("dp", "tensor"), scatter_dimension=0, tiled=True),
        lax.psum_scatter(new_parts[5], ("dp", "tensor"), scatter_dimension=0, tiled=True),
    )


def reduce_mlp(new_parts):
    return (
        lax.psum_scatter(new_parts[0], "dp", scatter_dimension=0, tiled=True),
        lax.psum_scatter(new_parts[1], "dp", scatter_dimension=0, tiled=True),
        lax.psum_scatter(new_parts[2], "dp", scatter_dimension=1, tiled=True),
    )


def accumulate(running, new_parts):
    if running is None:
        return tuple(new_parts)
    return tuple((earlier + latest for earlier, latest in zip(running, new_parts)))


def forward_block(inputs, seq_lengths, attn_full, mlp_full):
    first_gain, query_weight, key_weight, value_weight, output_weight, second_gain = attn_full
    gate_weight, up_weight, down_weight = mlp_full
    row_count = inputs.shape[0]
    group_size = HEADS // KV_HEADS
    factor = 1.0 / math.sqrt(HEAD)
    segment, position = pack_layout(seq_lengths, row_count)
    allowed = visible(segment, segment < SLOTS - 1)
    cosine, sine_part = rotary_tables(position, HEAD)
    first_scale = lax.rsqrt(jnp.mean(inputs * inputs, axis=1, keepdims=True) + EPSILON)
    normed_first = (inputs * first_scale * first_gain.astype(jnp.float32)).astype(jnp.bfloat16)
    queries = rotate(
        product(normed_first, query_weight).reshape(row_count, HEADS, HEAD), cosine, sine_part
    )
    queries = queries.astype(jnp.bfloat16).reshape(row_count, KV_HEADS, group_size, HEAD)
    key_vecs = rotate(
        product(normed_first, key_weight).reshape(row_count, KV_HEADS, HEAD), cosine, sine_part
    ).astype(jnp.bfloat16)
    values = (
        product(normed_first, value_weight).astype(jnp.bfloat16).reshape(row_count, KV_HEADS, HEAD)
    )
    scores = (
        jnp.einsum("qhgd,khd->hgqk", queries, key_vecs, preferred_element_type=jnp.float32) * factor
    )
    row_peak = jnp.max(jnp.where(allowed, scores, NEG_LARGE), axis=-1, keepdims=True)
    raised = jnp.where(allowed, jnp.exp(jnp.where(allowed, scores - row_peak, 0.0)), 0.0)
    totals = jnp.sum(raised, axis=-1, keepdims=True)
    safe_totals = jnp.where(totals > 0, totals, 1.0)
    log_total = row_peak + jnp.log(safe_totals)
    attn_probs = (raised / safe_totals).astype(jnp.bfloat16)
    blended = jnp.einsum("hgqk,khd->qhgd", attn_probs, values, preferred_element_type=jnp.float32)
    attended = blended.reshape(row_count, HEADS * HEAD).astype(jnp.bfloat16)
    middle = inputs + product(attended, output_weight)
    second_scale = lax.rsqrt(jnp.mean(middle * middle, axis=1, keepdims=True) + EPSILON)
    normed_second = (middle * second_scale * second_gain.astype(jnp.float32)).astype(jnp.bfloat16)
    gathered = lax.all_gather(normed_second, "tensor", axis=0, tiled=True)
    gate_pre = product(gathered, gate_weight)
    up_pre = product(gathered, up_weight)
    hidden = (jax.nn.silu(gate_pre) * up_pre).astype(jnp.bfloat16)
    layer_sum = middle + lax.psum_scatter(
        product(hidden, down_weight).astype(jnp.bfloat16), "tensor", scatter_dimension=0, tiled=True
    ).astype(jnp.float32)
    saved_state = (
        inputs,
        first_scale,
        normed_first,
        allowed,
        cosine,
        sine_part,
        queries,
        key_vecs,
        values,
        log_total,
        attended,
        middle,
        second_scale,
        gathered,
        gate_pre,
        up_pre,
        hidden,
    )
    return (layer_sum, saved_state)


def backward_block(upstream_low, saved_state, attn_full, mlp_full):
    (
        inputs,
        first_scale,
        normed_first,
        allowed,
        cosine,
        sine_part,
        queries,
        key_vecs,
        values,
        log_total,
        attended,
        middle,
        second_scale,
        gathered,
        gate_pre,
        up_pre,
        hidden,
    ) = saved_state
    first_gain, query_weight, key_weight, value_weight, output_weight, second_gain = attn_full
    gate_weight, up_weight, down_weight = mlp_full
    row_count = inputs.shape[0]
    group_size = HEADS // KV_HEADS
    factor = 1.0 / math.sqrt(HEAD)
    upstream = upstream_low.astype(jnp.float32)
    grad_gathered = lax.all_gather(upstream_low, "tensor", axis=0, tiled=True)
    hidden_grad = against(grad_gathered, down_weight)
    sig_gate = jax.nn.sigmoid(gate_pre)
    gate_grad = (hidden_grad * up_pre * sig_gate * (1.0 + gate_pre * (1.0 - sig_gate))).astype(
        jnp.bfloat16
    )
    up_grad = (hidden_grad * gate_pre * sig_gate).astype(jnp.bfloat16)
    mlp_parts = (
        across(gathered, gate_grad),
        across(gathered, up_grad),
        across(hidden, grad_gathered),
    )
    second_grad = lax.psum_scatter(
        against(gate_grad, gate_weight) + against(up_grad, up_weight),
        "tensor",
        scatter_dimension=0,
        tiled=True,
    )
    middle_part, second_gain_grad = norm_back(
        second_grad, middle, second_scale, second_gain.astype(jnp.float32)
    )
    middle_grad = upstream + middle_part
    middle_low = middle_grad.astype(jnp.bfloat16)
    output_part = across(attended, middle_low)
    attended_grad = (
        against(middle_low, output_weight)
        .astype(jnp.bfloat16)
        .reshape(row_count, KV_HEADS, group_size, HEAD)
    )
    scores = (
        jnp.einsum("qhgd,khd->hgqk", queries, key_vecs, preferred_element_type=jnp.float32) * factor
    )
    attn_probs = jnp.where(allowed, jnp.exp(jnp.where(allowed, scores - log_total, 0.0)), 0.0)
    prob_grad = jnp.einsum(
        "qhgd,khd->hgqk", attended_grad, values, preferred_element_type=jnp.float32
    )
    delta_sum = jnp.sum(attn_probs * prob_grad, axis=-1, keepdims=True)
    score_grad = (attn_probs * (prob_grad - delta_sum)).astype(jnp.bfloat16)
    value_grad = jnp.einsum(
        "hgqk,qhgd->khd",
        attn_probs.astype(jnp.bfloat16),
        attended_grad,
        preferred_element_type=jnp.float32,
    )
    value_grad = value_grad.astype(jnp.bfloat16).reshape(row_count, KV_HEADS * HEAD)
    query_rot_grad = (
        jnp.einsum("hgqk,khd->qhgd", score_grad, key_vecs, preferred_element_type=jnp.float32)
        * factor
    )
    key_rot_grad = (
        jnp.einsum("hgqk,qhgd->khd", score_grad, queries, preferred_element_type=jnp.float32)
        * factor
    )
    query_grad = (
        unrotate(query_rot_grad.reshape(row_count, HEADS, HEAD), cosine, sine_part)
        .astype(jnp.bfloat16)
        .reshape(row_count, HEADS * HEAD)
    )
    key_grad = (
        unrotate(key_rot_grad, cosine, sine_part)
        .astype(jnp.bfloat16)
        .reshape(row_count, KV_HEADS * HEAD)
    )
    first_grad = (
        against(query_grad, query_weight)
        + against(key_grad, key_weight)
        + against(value_grad, value_weight)
    )
    input_part, first_gain_grad = norm_back(
        first_grad, inputs, first_scale, first_gain.astype(jnp.float32)
    )
    input_grad = middle_grad + input_part
    attn_parts = (
        first_gain_grad,
        across(normed_first, query_grad),
        across(normed_first, key_grad),
        across(normed_first, value_grad),
        output_part,
        second_gain_grad,
    )
    return (input_grad, attn_parts, mlp_parts)


def per_device(
    tokens,
    lengths,
    first_gain,
    query_weight,
    key_weight,
    value_weight,
    output_weight,
    second_gain,
    gate_weight,
    up_weight,
    down_weight,
    cotangent,
):
    micro_count = tokens.shape[0]
    outputs = []
    input_grads = []
    attn_total = None
    mlp_total = None
    for step_index in range(micro_count):
        attn_full = fetch_attention(
            first_gain, query_weight, key_weight, value_weight, output_weight, second_gain
        )
        mlp_full = fetch_mlp(gate_weight, up_weight, down_weight)
        layer_sum, saved_state = forward_block(
            tokens[step_index].astype(jnp.float32), lengths[step_index, 0], attn_full, mlp_full
        )
        outputs.append(layer_sum.astype(jnp.bfloat16))
        input_grad, attn_parts, mlp_parts = backward_block(
            cotangent[step_index], saved_state, attn_full, mlp_full
        )
        input_grads.append(input_grad)
        attn_parts = reduce_attention(attn_parts)
        mlp_parts = reduce_mlp(mlp_parts)
        attn_total = accumulate(attn_total, attn_parts)
        mlp_total = accumulate(mlp_total, mlp_parts)
    return (
        jnp.stack(outputs),
        jnp.stack(input_grads),
        attn_total[0],
        attn_total[1],
        attn_total[2],
        attn_total[3],
        attn_total[4],
        attn_total[5],
        mlp_total[0],
        mlp_total[1],
        mlp_total[2],
    )


def solution(mesh):
    placed = (
        P(None, ("dp", "tensor"), None),
        P(None, ("dp", "tensor"), None),
        P(("dp", "tensor")),
        P(("dp", "tensor"), None),
        P(("dp", "tensor"), None),
        P(("dp", "tensor"), None),
        P(("dp", "tensor"), None),
        P(("dp", "tensor")),
        P("dp", "tensor"),
        P("dp", "tensor"),
        P("tensor", "dp"),
        P(None, ("dp", "tensor"), None),
    )
    return jax.shard_map(
        per_device,
        mesh=mesh,
        in_specs=placed,
        out_specs=(
            P(None, ("dp", "tensor"), None),
            P(None, ("dp", "tensor"), None),
            P(("dp", "tensor")),
            P(("dp", "tensor"), None),
            P(("dp", "tensor"), None),
            P(("dp", "tensor"), None),
            P(("dp", "tensor"), None),
            P(("dp", "tensor")),
            P("dp", "tensor"),
            P("dp", "tensor"),
            P("tensor", "dp"),
        ),
        check_vma=False,
    )
```

profile of v0, /device:TPU:0, one launch (start us, length us, event | category | flops | bytes accessed | tf_op | source)
XLA Modules:
  0.0 1699.0 jit_solution(15163263010389915065)
XLA Ops:
  14.5 42.2 %all-reduce.5 = (bf16[1536]{0:T(1024)(128)(2,1)S(1)}, bf16[1536]{0:T(1024)(128)(2,1)S(1)}) all-reduce(bf16[1536]{0:T(1024)(128)(2,1)S(1)} %dynamic-update-slice, bf16[1536]{0:T(1024)(128)(2,1)S(1)} %dynamic-update-slice.1), channel_id=1, replica_groups=mesh['dp'=8,'tensor'=4] {'dp','tensor'}, use_global_device_ids=true, to_apply=%add | all-reduce | flops 3072 | bytes 12288
  61.2 9.6 all-gather.17.cloned.1.call-done
  74.0 55.8 %all-gather.19.cloned.1.call-done = bf16[1536,768]{1,0:T(8,128)(2,1)} async-done(((bf16[48,768]{1,0:T(8,128)(2,1)}), bf16[1536,768]{1,0:T(8,128)(2,1)}) %all-gather.19.cloned.1.call-update) | async-done | bytes 2359312 | tf_op jit(solution)/shard_map/all_gather | solution.py:99
  135.1 60.2 %all-gather.21.cloned.1.call-done = bf16[1536,1536]{1,0:T(8,128)(2,1)} async-done(((bf16[48,1536]{1,0:T(8,128)(2,1)}), bf16[1536,1536]{1,0:T(8,128)(2,1)}) %all-gather.21.cloned.1.call-update) | async-done | bytes 4718608 | tf_op jit(solution)/shard_map/all_gather | solution.py:98
  207.8 52.7 %all-gather.23.cloned.1.call-done = bf16[1536,1536]{1,0:T(8,128)(2,1)} async-done(((bf16[48,1536]{1,0:T(8,128)(2,1)}), bf16[1536,1536]{1,0:T(8,128)(2,1)}) %all-gather.23.cloned.1.call-update) | async-done | bytes 4718608 | tf_op jit(solution)/shard_map/all_gather | solution.py:101
  268.4 53.5 %all-gather.29.cloned.1.call-done = bf16[1536,1024]{1,0:T(8,128)(2,1)} async-done(((bf16[192,1024]{1,0:T(8,128)(2,1)}), bf16[1536,1024]{1,0:T(8,128)(2,1)}) %all-gather.29.cloned.1.call-update) | async-done | bytes 3145744 | tf_op jit(solution)/shard_map/all_gather | solution.py:109
  321.9 20.3 %all-gather.25.cloned.1.call-done = bf16[512,1536]{1,0:T(8,128)(2,1)} async-done(((bf16[128,1536]{1,0:T(8,128)(2,1)}), bf16[512,1536]{1,0:T(8,128)(2,1)}) %all-gather.25.cloned.1.call-update) | async-done | bytes 1572880 | tf_op jit(solution)/shard_map/all_gather | solution.py:174
  347.7 57.1 %all-gather.27.cloned.1.call-done = bf16[1536,1024]{1,0:T(8,128)(2,1)} async-done(((bf16[192,1024]{1,0:T(8,128)(2,1)}), bf16[1536,1024]{1,0:T(8,128)(2,1)}) %all-gather.27.cloned.1.call-update) | async-done | bytes 3145744 | tf_op jit(solution)/shard_map/all_gather | solution.py:108
  409.9 15.4 all-gather.37.cloned.1.call-done
  425.3 62.7 %all-gather.31.cloned.1.call-done = bf16[1024,1536]{0,1:T(8,128)(2,1)} async-done(((bf16[1024,192]{0,1:T(8,128)(2,1)}), bf16[1024,1536]{0,1:T(8,128)(2,1)}) %all-gather.31.cloned.1.call-update) | async-done | bytes 3145744 | tf_op jit(solution)/shard_map/all_gather | solution.py:110
  531.1 35.7 %reduce-scatter.20.cloned.1.call-done = f32[128,1536]{1,0:T(8,128)} async-done(((f32[512,1536]{1,0:T(8,128)}), f32[128,1536]{1,0:T(8,128)}) %reduce-scatter.20.cloned.1.call-update) | async-done | bytes 786448 | tf_op jit(solution)/shard_map/reduce_scatter | solution.py:241
  572.2 17.7 %all-gather.35.cloned.1.call-done = bf16[512,1536]{1,0:T(8,128)(2,1)} async-done(((bf16[128,1536]{1,0:T(8,128)(2,1)}), bf16[512,1536]{1,0:T(8,128)(2,1)}) %all-gather.35.cloned.1.call-update) | async-done | bytes 1572880 | tf_op jit(solution)/shard_map/all_gather | solution.py:174
  598.6 13.0 all-gather.41.cloned.1.call-done
  641.6 12.3 all-gather.39.cloned.1.call-done
  684.4 31.3 %reduce-scatter.16.cloned.1.call-done = bf16[128,1536]{1,0:T(8,128)(2,1)} async-done(((bf16[512,1536]{1,0:T(8,128)(2,1)}), bf16[128,1536]{1,0:T(8,128)(2,1)}) %reduce-scatter.16.cloned.1.call-update) | async-done | bytes 393232 | tf_op jit(solution)/shard_map/reduce_scatter | solution.py:178
  715.7 40.4 %reduce-scatter.22.cloned.1.call-done = f32[128,1536]{1,0:T(8,128)} async-done(((f32[512,1536]{1,0:T(8,128)}), f32[128,1536]{1,0:T(8,128)}) %reduce-scatter.22.cloned.1.call-update) | async-done | bytes 786448 | tf_op jit(solution)/shard_map/reduce_scatter | solution.py:241
  756.1 40.7 %reduce-scatter.24.cloned.1.call-done = f32[128,1536]{1,0:T(8,128)} async-done(((f32[512,1536]{1,0:T(8,128)}), f32[128,1536]{1,0:T(8,128)}) %reduce-scatter.24.cloned.1.call-update) | async-done | bytes 786448 | tf_op jit(solution)/shard_map/reduce_scatter | solution.py:241
  909.6 39.9 %all-reduce.4 = (f32[1536]{0:T(1024)}, f32[1536]{0:T(1024)}) all-reduce(f32[1536]{0:T(1024)} %add_add_fusion.6, f32[1536]{0:T(1024)S(1)} %copy-done.131), channel_id=29, replica_groups=mesh['dp'=8,'tensor'=4] {'dp','tensor'}, use_global_device_ids=true, to_apply=%region_37.38.clone | all-reduce | flops 3072 | bytes 24576
  960.3 85.1 %reduce-scatter.28.cloned.1.call-done = f32[48,768]{1,0:T(8,128)} async-done(((f32[1536,768]{1,0:T(8,128)}), f32[48,768]{1,0:T(8,128)}) %reduce-scatter.28.cloned.1.call-update) | async-done | bytes 147472 | tf_op jit(solution)/shard_map/reduce_scatter | solution.py:118
  1045.4 121.3 %reduce-scatter.38.cloned.1.call-done = f32[1024,192]{0,1:T(8,128)} async-done(((f32[1024,1536]{0,1:T(8,128)}), f32[1024,192]{0,1:T(8,128)}) %reduce-scatter.38.cloned.1.call-update) | async-done | bytes 786448 | tf_op jit(solution)/shard_map/reduce_scatter | solution.py:129
  1166.7 121.3 %reduce-scatter.36.cloned.1.call-done = f32[192,1024]{1,0:T(8,128)} async-done(((f32[1536,1024]{1,0:T(8,128)}), f32[192,1024]{1,0:T(8,128)}) %reduce-scatter.36.cloned.1.call-update) | async-done | bytes 786448 | tf_op jit(solution)/shard_map/reduce_scatter | solution.py:128
  1288.0 121.1 %reduce-scatter.34.cloned.1.call-done = f32[192,1024]{1,0:T(8,128)} async-done(((f32[1536,1024]{1,0:T(8,128)}), f32[192,1024]{1,0:T(8,128)}) %reduce-scatter.34.cloned.1.call-update) | async-done | bytes 786448 | tf_op jit(solution)/shard_map/reduce_scatter | solution.py:127
  1409.2 141.2 %reduce-scatter.32.cloned.1.call-done = f32[48,1536]{1,0:T(8,128)} async-done(((f32[1536,1536]{1,0:T(8,128)}), f32[48,1536]{1,0:T(8,128)}) %reduce-scatter.32.cloned.1.call-update) | async-done | bytes 294928 | tf_op jit(solution)/shard_map/reduce_scatter | solution.py:120
  1550.3 142.0 %reduce-scatter.26.cloned.1.call-done = f32[48,1536]{1,0:T(8,128)} async-done(((f32[1536,1536]{1,0:T(8,128)}), f32[48,1536]{1,0:T(8,128)}) %reduce-scatter.26.cloned.1.call-update) | async-done | bytes 294928 | tf_op jit(solution)/shard_map/reduce_scatter | solution.py:117
  (615 shorter events, 289.8 us)
Async XLA Ops:
  7.2 63.7 %all-gather.17.cloned.1.call-start = ((), (), s32[]{:S(2)}) async-start(), calls=%async_computation.13 | async-start | bytes 2433024 | tf_op jit(solution)/shard_map/all_gather | solution.py:100
  7.9 121.9 %all-gather.19.cloned.1.call-start = ((), (), s32[]{:S(2)}) async-start(), calls=%async_computation.14 | async-start | bytes 2433024 | tf_op jit(solution)/shard_map/all_gather | solution.py:99
  8.7 186.6 %all-gather.21.cloned.1.call-start = ((), (), s32[]{:S(2)}) async-start(), calls=%async_computation.15 | async-start | bytes 4866048 | tf_op jit(solution)/shard_map/all_gather | solution.py:98
  9.4 251.1 %all-gather.23.cloned.1.call-start = ((), (), s32[]{:S(2)}) async-start(), calls=%async_computation.16 | async-start | bytes 4866048 | tf_op jit(solution)/shard_map/all_gather | solution.py:101
  10.0 311.9 %all-gather.29.cloned.1.call-start = ((), (), s32[]{:S(2)}) async-start(), calls=%async_computation.19 | async-start | bytes 3538944 | tf_op jit(solution)/shard_map/all_gather | solution.py:109
  10.6 331.6 %all-gather.25.cloned.1.call-start = ((), (), s32[]{:S(2)}) async-start(), calls=%async_computation.17 | async-start | bytes 1966080 | tf_op jit(solution)/shard_map/all_gather | solution.py:174
  265.2 139.6 %all-gather.27.cloned.1.call-start = ((), (), s32[]{:S(2)}) async-start(), calls=%async_computation.18 | async-start | bytes 3538944 | tf_op jit(solution)/shard_map/all_gather | solution.py:108
  266.0 159.3 %all-gather.37.cloned.1.call-start = ((), (), s32[]{:S(2)}) async-start(), calls=%async_computation.29 | async-start | bytes 1966080 | tf_op jit(solution)/shard_map/all_gather | solution.py:229
  267.1 220.8 %all-gather.31.cloned.1.call-start = ((), (), s32[]{:S(2)}) async-start(), calls=%async_computation.20 | async-start | bytes 3538944 | tf_op jit(solution)/shard_map/all_gather | solution.py:110
  267.9 263.2 %reduce-scatter.14.cloned.1.call-start = ((), (), s32[]{:S(2)}) async-start(), calls=%async_computation.21 | async-start | bytes 1966080 | tf_op jit(solution)/shard_map/reduce_scatter | solution.py:178
  499.2 67.6 %reduce-scatter.20.cloned.1.call-start = ((), (), s32[]{:S(2)}) async-start(), calls=%async_computation.26 | async-start | bytes 3932160 | tf_op jit(solution)/shard_map/reduce_scatter | solution.py:241
  507.9 81.9 %all-gather.35.cloned.1.call-start = ((), (), s32[]{:S(2)}) async-start(), calls=%async_computation.24 | async-start | bytes 1966080 | tf_op jit(solution)/shard_map/all_gather | solution.py:174
  571.3 82.5 %all-gather.39.cloned.1.call-start = ((), (), s32[]{:S(2)}) async-start(), calls=%async_computation.30 | async-start | bytes 1966080 | tf_op jit(solution)/shard_map/all_gather | solution.py:229
  571.9 112.5 %reduce-scatter.18.cloned.1.call-start = ((), (), s32[]{:S(2)}) async-start(), calls=%async_computation.25 | async-start | bytes 1966080 | tf_op jit(solution)/shard_map/reduce_scatter | solution.py:178
  623.4 92.3 %reduce-scatter.16.cloned.1.call-start = ((), (), s32[]{:S(2)}) async-start(), calls=%async_computation.23 | async-start | bytes 1966080 | tf_op jit(solution)/shard_map/reduce_scatter | solution.py:178
  665.4 90.7 %reduce-scatter.22.cloned.1.call-start = ((), (), s32[]{:S(2)}) async-start(), calls=%async_computation.27 | async-start | bytes 3932160 | tf_op jit(solution)/shard_map/reduce_scatter | solution.py:241
  673.7 123.1 %reduce-scatter.24.cloned.1.call-start = ((), (), s32[]{:S(2)}) async-start(), calls=%async_computation.28 | async-start | bytes 3932160 | tf_op jit(solution)/shard_map/reduce_scatter | solution.py:241
  681.6 278.7 %reduce-scatter.30.cloned.1.call-start = ((), (), s32[]{:S(2)}) async-start(), calls=%async_computation.34 | async-start | bytes 4866048 | tf_op jit(solution)/shard_map/reduce_scatter | solution.py:119
  825.1 220.4 %reduce-scatter.28.cloned.1.call-start = ((), (), s32[]{:S(2)}) async-start(), calls=%async_computation.33 | async-start | bytes 4866048 | tf_op jit(solution)/shard_map/reduce_scatter | solution.py:118
  837.9 328.8 %reduce-scatter.38.cloned.1.call-start = ((), (), s32[]{:S(2)}) async-start(), calls=%async_computation.38 | async-start | bytes 7077888 | tf_op jit(solution)/shard_map/reduce_scatter | solution.py:129
  848.5 439.5 %reduce-scatter.36.cloned.1.call-start = ((), (), s32[]{:S(2)}) async-start(), calls=%async_computation.37 | async-start | bytes 7077888 | tf_op jit(solution)/shard_map/reduce_scatter | solution.py:128
  859.3 549.8 %reduce-scatter.34.cloned.1.call-start = ((), (), s32[]{:S(2)}) async-start(), calls=%async_computation.36 | async-start | bytes 7077888 | tf_op jit(solution)/shard_map/reduce_scatter | solution.py:127
  869.7 680.6 %reduce-scatter.32.cloned.1.call-start = ((), (), s32[]{:S(2)}) async-start(), calls=%async_computation.35 | async-start | bytes 9732096 | tf_op jit(solution)/shard_map/reduce_scatter | solution.py:120
  879.8 812.5 %reduce-scatter.26.cloned.1.call-start = ((), (), s32[]{:S(2)}) async-start(), calls=%async_computation.32 | async-start | bytes 9732096 | tf_op jit(solution)/shard_map/reduce_scatter | solution.py:117
  (196 other events, 1816.7 us)
Sparse Core Ops, SparseCore 0:
  10.9 59.9 all-gather.16
  73.8 56.0 all-gather.18
  132.7 62.5 all-gather.20
  198.1 62.4 all-gather.22
  262.6 59.2 all-gather.28
  344.3 60.4 all-gather.26
  427.5 60.4 all-gather.30
  499.3 26.7 reduce-scatter.13
  528.8 37.9 reduce-scatter.19
  570.1 19.6 all-gather.34
  591.9 19.6 all-gather.40
  613.1 19.6 all-gather.32
  634.2 19.6 all-gather.38
  656.2 28.1 reduce-scatter.17
  687.6 28.1 reduce-scatter.15
  718.1 37.9 reduce-scatter.21
  758.8 37.9 reduce-scatter.23
  825.2 107.0 reduce-scatter.29
  939.2 106.1 reduce-scatter.27
  1049.6 117.0 reduce-scatter.37
  1170.9 117.0 reduce-scatter.35
  1292.0 117.0 reduce-scatter.33
  1415.6 134.6 reduce-scatter.31
  1557.6 134.5 reduce-scatter.25
  (2 shorter events, 36.4 us)
where the time goes:
time: 1710 us; the launch traced here: 1700 us
  waiting for transfers between devices  1330 us (78%)
  matrix products  200 us (12%)
  blocking collectives  82.1 us (5%)
  other arithmetic  37.4 us (2%)
  local copies, waits for them, and re-layouts  32.3 us (2%)
    reduce_scatter x1, waiting for transfers between devices, reduce_attention(): lax.psum_scatter(new_parts[1], ('dp', 'tensor'), scatter_dimension=0, til...  142 us
    reduce_scatter x1, waiting for transfers between devices, reduce_attention(): lax.psum_scatter(new_parts[4], ('dp', 'tensor'), scatter_dimension=0, til...  141 us
    reduce_scatter x1, waiting for transfers between devices, reduce_mlp(): lax.psum_scatter(new_parts[1], 'dp', scatter_dimension=0, tiled=True)  121 us
    reduce_scatter x1, waiting for transfers between devices, reduce_mlp(): lax.psum_scatter(new_parts[2], 'dp', scatter_dimension=1, tiled=True)  121 us
    reduce_scatter x1, waiting for transfers between devices, reduce_mlp(): lax.psum_scatter(new_parts[0], 'dp', scatter_dimension=0, tiled=True)  121 us
    reduce_scatter x3, waiting for transfers between devices, backward_block(): lax.psum_scatter(against(gate_grad, gate_weight) + against(up_grad, up_we...  117 us
    reduce_scatter x1, waiting for transfers between devices, reduce_attention(): lax.psum_scatter(new_parts[2], ('dp', 'tensor'), scatter_dimension=0, til...  85.1 us
    unnamed x2, blocking collectives  82.1 us
  transfers between devices with their start and end apart: 26, of which 24 were waited for; matrix products, arithmetic and copies ran while one was open for 13% of the time, Pallas kernels for 0%

commit v1 on v0

--- a/solution.py
+++ b/solution.py
@@ -171,7 +171,14 @@
     middle = inputs + product(attended, output_weight)
     second_scale = lax.rsqrt(jnp.mean(middle * middle, axis=1, keepdims=True) + EPSILON)
     normed_second = (middle * second_scale * second_gain.astype(jnp.float32)).astype(jnp.bfloat16)
-    gathered = lax.all_gather(normed_second, "tensor", axis=0, tiled=True)
+    ring = [normed_second]
+    for hop in range(3):
+        ring.append(lax.ppermute(ring[-1], "tensor", [(dev, (dev + 1) % 4) for dev in range(4)]))
+    gathered = jnp.roll(
+        jnp.concatenate(ring[::-1], axis=0),
+        (lax.axis_index("tensor") + 1) * ring[0].shape[0],
+        axis=0,
+    )
     gate_pre = product(gathered, gate_weight)
     up_pre = product(gathered, up_weight)
     hidden = (jax.nn.silu(gate_pre) * up_pre).astype(jnp.bfloat16)

time: 1710 us -> 1660 us (0.971)
  waiting for transfers between devices: 1330 us -> 1250 us
  other arithmetic: 37.4 us -> 57.4 us
    all_gather x3 -> x0, waiting for transfers between devices: 47.3 us -> none  [forward_block(): gathered = lax.all_gather(normed_second, 'tensor', axis=0, tiled=True)]
    ppermute x0 -> x9, waiting for transfers between devices: none -> 45.1 us  [forward_block(): lax.ppermute(ring[-1], 'tensor', [(dev, (dev + 1) % 4) for dev in range(4)])]
    all_gather x3, waiting for transfers between devices: 40.7 us -> 0.37 us  [backward_block(): grad_gathered = lax.all_gather(upstream_low, 'tensor', axis=0, tiled=True)]
  transfers between devices with their start and end apart: 26 -> 32, of which waited for: 24 -> 24; matrix products, arithmetic and copies ran while one was open for 13% -> 14% of each run, Pallas kernels for 0% -> 0%
where the time goes in v1:
time: 1660 us; the launch traced here: 1650 us
  waiting for transfers between devices  1250 us (75%)
  matrix products  190 us (11%)
  blocking collectives  82.2 us (5%)
  other arithmetic  57.4 us (3%)
  local copies, waits for them, and re-layouts  38.9 us (2%)
  between operations  17.1 us (1%)
  starting transfers between devices  16.6 us (1%)
    reduce_scatter x1, waiting for transfers between devices, reduce_attention(): lax.psum_scatter(new_parts[1], ('dp', 'tensor'), scatter_dimension=0, til...  142 us
    reduce_scatter x1, waiting for transfers between devices, reduce_attention(): lax.psum_scatter(new_parts[4], ('dp', 'tensor'), scatter_dimension=0, til...  141 us
    reduce_scatter x1, waiting for transfers between devices, reduce_mlp(): lax.psum_scatter(new_parts[2], 'dp', scatter_dimension=1, tiled=True)  121 us
    reduce_scatter x1, waiting for transfers between devices, reduce_mlp(): lax.psum_scatter(new_parts[0], 'dp', scatter_dimension=0, tiled=True)  121 us
    reduce_scatter x1, waiting for transfers between devices, reduce_mlp(): lax.psum_scatter(new_parts[1], 'dp', scatter_dimension=0, tiled=True)  121 us
    reduce_scatter x3, waiting for transfers between devices, backward_block(): lax.psum_scatter(against(gate_grad, gate_weight) + against(up_grad, up_we...  100 us
    reduce_scatter x1, waiting for transfers between devices, reduce_attention(): lax.psum_scatter(new_parts[2], ('dp', 'tensor'), scatter_dimension=0, til...  86.2 us
    unnamed x2, blocking collectives  82.2 us
  transfers between devices with their start and end apart: 32, of which 24 were waited for; matrix products, arithmetic and copies ran while one was open for 14% of the time, Pallas kernels for 0%

profile of v1, /device:TPU:0, one launch (start us, length us, event | category | flops | bytes accessed | tf_op | source)
XLA Modules:
  0.0 1648.0 jit_solution(7400816539513562640)
XLA Ops:
  17.8 42.1 %all-reduce.5 = (bf16[1536]{0:T(1024)(128)(2,1)S(1)}, bf16[1536]{0:T(1024)(128)(2,1)S(1)}) all-reduce(bf16[1536]{0:T(1024)(128)(2,1)S(1)} %dynamic-update-slice, bf16[1536]{0:T(1024)(128)(2,1)S(1)} %dynamic-update-slice.1), channel_id=1, replica_groups=mesh['dp'=8,'tensor'=4] {'dp','tensor'}, use_global_device_ids=true, to_apply=%add | all-reduce | flops 3072 | bytes 12288
  61.6 9.5 all-gather.14.cloned.1.call-done
  74.1 55.9 %all-gather.16.cloned.1.call-done = bf16[1536,768]{1,0:T(8,128)(2,1)} async-done(((bf16[48,768]{1,0:T(8,128)(2,1)}), bf16[1536,768]{1,0:T(8,128)(2,1)}) %all-gather.16.cloned.1.call-update) | async-done | bytes 2359312 | tf_op jit(solution)/shard_map/all_gather | solution.py:99
  135.2 60.3 %all-gather.18.cloned.1.call-done = bf16[1536,1536]{1,0:T(8,128)(2,1)} async-done(((bf16[48,1536]{1,0:T(8,128)(2,1)}), bf16[1536,1536]{1,0:T(8,128)(2,1)}) %all-gather.18.cloned.1.call-update) | async-done | bytes 4718608 | tf_op jit(solution)/shard_map/all_gather | solution.py:98
  209.4 51.3 %all-gather.20.cloned.1.call-done = bf16[1536,1536]{1,0:T(8,128)(2,1)} async-done(((bf16[48,1536]{1,0:T(8,128)(2,1)}), bf16[1536,1536]{1,0:T(8,128)(2,1)}) %all-gather.20.cloned.1.call-update) | async-done | bytes 4718608 | tf_op jit(solution)/shard_map/all_gather | solution.py:101
  266.2 10.5 collective-permute-done
  277.9 8.0 collective-permute-done.1
  286.1 60.3 %all-gather.26.cloned.1.call-done = bf16[1024,1536]{0,1:T(8,128)(2,1)} async-done(((bf16[1024,192]{0,1:T(8,128)(2,1)}), bf16[1024,1536]{0,1:T(8,128)(2,1)}) %all-gather.26.cloned.1.call-update) | async-done | bytes 3145744 | tf_op jit(solution)/shard_map/all_gather | solution.py:110
  358.5 49.2 %all-gather.24.cloned.1.call-done = bf16[1536,1024]{1,0:T(8,128)(2,1)} async-done(((bf16[192,1024]{1,0:T(8,128)(2,1)}), bf16[1536,1024]{1,0:T(8,128)(2,1)}) %all-gather.24.cloned.1.call-update) | async-done | bytes 3145744 | tf_op jit(solution)/shard_map/all_gather | solution.py:109
  413.2 55.8 %all-gather.22.cloned.1.call-done = bf16[1536,1024]{1,0:T(8,128)(2,1)} async-done(((bf16[192,1024]{1,0:T(8,128)(2,1)}), bf16[1536,1024]{1,0:T(8,128)(2,1)}) %all-gather.22.cloned.1.call-update) | async-done | bytes 3145744 | tf_op jit(solution)/shard_map/all_gather | solution.py:108
  469.0 7.7 multiply_convert_fusion.4
  489.2 11.7 all-gather.30.cloned.1.call-start
  528.9 19.2 %reduce-scatter.20.cloned.1.call-done = f32[128,1536]{1,0:T(8,128)} async-done(((f32[512,1536]{1,0:T(8,128)}), f32[128,1536]{1,0:T(8,128)}) %reduce-scatter.20.cloned.1.call-update) | async-done | bytes 786448 | tf_op jit(solution)/shard_map/reduce_scatter | solution.py:248
  559.6 12.5 collective-permute-done.7
  637.1 19.6 %reduce-scatter.16.cloned.1.call-done = bf16[128,1536]{1,0:T(8,128)(2,1)} async-done(((bf16[512,1536]{1,0:T(8,128)(2,1)}), bf16[128,1536]{1,0:T(8,128)(2,1)}) %reduce-scatter.16.cloned.1.call-update) | async-done | bytes 393232 | tf_op jit(solution)/shard_map/reduce_scatter | solution.py:185
  656.7 40.3 %reduce-scatter.22.cloned.1.call-done = f32[128,1536]{1,0:T(8,128)} async-done(((f32[512,1536]{1,0:T(8,128)}), f32[128,1536]{1,0:T(8,128)}) %reduce-scatter.22.cloned.1.call-update) | async-done | bytes 786448 | tf_op jit(solution)/shard_map/reduce_scatter | solution.py:248
  697.1 40.5 %reduce-scatter.24.cloned.1.call-done = f32[128,1536]{1,0:T(8,128)} async-done(((f32[512,1536]{1,0:T(8,128)}), f32[128,1536]{1,0:T(8,128)}) %reduce-scatter.24.cloned.1.call-update) | async-done | bytes 786448 | tf_op jit(solution)/shard_map/reduce_scatter | solution.py:248
  857.0 40.0 %all-reduce.4 = (f32[1536]{0:T(1024)}, f32[1536]{0:T(1024)}) all-reduce(f32[1536]{0:T(1024)} %add_add_fusion.6, f32[1536]{0:T(1024)S(1)} %copy-done.136), channel_id=29, replica_groups=mesh['dp'=8,'tensor'=4] {'dp','tensor'}, use_global_device_ids=true, to_apply=%region_37.39.clone | all-reduce | flops 3072 | bytes 24576
  907.8 86.2 %reduce-scatter.28.cloned.1.call-done = f32[48,768]{1,0:T(8,128)} async-done(((f32[1536,768]{1,0:T(8,128)}), f32[48,768]{1,0:T(8,128)}) %reduce-scatter.28.cloned.1.call-update) | async-done | bytes 147472 | tf_op jit(solution)/shard_map/reduce_scatter | solution.py:118
  993.9 121.3 %reduce-scatter.38.cloned.1.call-done = f32[1024,192]{0,1:T(8,128)} async-done(((f32[1024,1536]{0,1:T(8,128)}), f32[1024,192]{0,1:T(8,128)}) %reduce-scatter.38.cloned.1.call-update) | async-done | bytes 786448 | tf_op jit(solution)/shard_map/reduce_scatter | solution.py:129
  1115.2 121.1 %reduce-scatter.36.cloned.1.call-done = f32[192,1024]{1,0:T(8,128)} async-done(((f32[1536,1024]{1,0:T(8,128)}), f32[192,1024]{1,0:T(8,128)}) %reduce-scatter.36.cloned.1.call-update) | async-done | bytes 786448 | tf_op jit(solution)/shard_map/reduce_scatter | solution.py:128
  1236.4 121.3 %reduce-scatter.34.cloned.1.call-done = f32[192,1024]{1,0:T(8,128)} async-done(((f32[1536,1024]{1,0:T(8,128)}), f32[192,1024]{1,0:T(8,128)}) %reduce-scatter.34.cloned.1.call-update) | async-done | bytes 786448 | tf_op jit(solution)/shard_map/reduce_scatter | solution.py:127
  1357.7 141.0 %reduce-scatter.32.cloned.1.call-done = f32[48,1536]{1,0:T(8,128)} async-done(((f32[1536,1536]{1,0:T(8,128)}), f32[48,1536]{1,0:T(8,128)}) %reduce-scatter.32.cloned.1.call-update) | async-done | bytes 294928 | tf_op jit(solution)/shard_map/reduce_scatter | solution.py:120
  1498.7 142.4 %reduce-scatter.26.cloned.1.call-done = f32[48,1536]{1,0:T(8,128)} async-done(((f32[1536,1536]{1,0:T(8,128)}), f32[48,1536]{1,0:T(8,128)}) %reduce-scatter.26.cloned.1.call-update) | async-done | bytes 294928 | tf_op jit(solution)/shard_map/reduce_scatter | solution.py:117
  (619 shorter events, 302.9 us)
Async XLA Ops:
  7.2 63.9 %all-gather.14.cloned.1.call-start = ((), (), s32[]{:S(2)}) async-start(), calls=%async_computation.13 | async-start | bytes 2433024 | tf_op jit(solution)/shard_map/all_gather | solution.py:100
  8.0 122.1 %all-gather.16.cloned.1.call-start = ((), (), s32[]{:S(2)}) async-start(), calls=%async_computation.14 | async-start | bytes 2433024 | tf_op jit(solution)/shard_map/all_gather | solution.py:99
  8.7 186.8 %all-gather.18.cloned.1.call-start = ((), (), s32[]{:S(2)}) async-start(), calls=%async_computation.15 | async-start | bytes 4866048 | tf_op jit(solution)/shard_map/all_gather | solution.py:98
  9.4 251.3 %all-gather.20.cloned.1.call-start = ((), (), s32[]{:S(2)}) async-start(), calls=%async_computation.16 | async-start | bytes 4866048 | tf_op jit(solution)/shard_map/all_gather | solution.py:101
  10.0 276.1 %all-gather.28.cloned.1.call-start = ((), (), s32[]{:S(2)}) async-start(), calls=%async_computation.26 | async-start | bytes 1966080 | tf_op jit(solution)/shard_map/all_gather | solution.py:236
  12.4 334.0 %all-gather.26.cloned.1.call-start = ((), (), s32[]{:S(2)}) async-start(), calls=%async_computation.19 | async-start | bytes 3538944 | tf_op jit(solution)/shard_map/all_gather | solution.py:110
  13.0 394.7 %all-gather.24.cloned.1.call-start = ((), (), s32[]{:S(2)}) async-start(), calls=%async_computation.18 | async-start | bytes 3538944 | tf_op jit(solution)/shard_map/all_gather | solution.py:109
  13.7 455.3 %all-gather.22.cloned.1.call-start = ((), (), s32[]{:S(2)}) async-start(), calls=%async_computation.17 | async-start | bytes 3538944 | tf_op jit(solution)/shard_map/all_gather | solution.py:108
  14.5 514.4 %reduce-scatter.14.cloned.1.call-start = ((), (), s32[]{:S(2)}) async-start(), calls=%async_computation.20 | async-start | bytes 1966080 | tf_op jit(solution)/shard_map/reduce_scatter | solution.py:185
  285.9 66.1 %collective-permute-start.2 = (bf16[128,1536]{1,0:T(8,128)(2,1)}, bf16[128,1536]{1,0:T(8,128)(2,1)}, u32[]{:S(2)}, u32[]{:S(2)}) collective-permute-start(bf16[128,1536]{1,0:T(8,128)(2,1)} %collective-permute-done.1), channel_id=1, source_target_pairs={{0,1},{1,2},{2,3},{3,0},{4,5},{5,6},{6,7},{7,4},{8,9},{9,10},{10,1... | collective-permute-start | bytes 1179656 | tf_op jit(solution)/shard_map/ppermute | solution.py:176
  480.6 67.5 %reduce-scatter.20.cloned.1.call-start = ((), (), s32[]{:S(2)}) async-start(), calls=%async_computation.23 | async-start | bytes 3932160 | tf_op jit(solution)/shard_map/reduce_scatter | solution.py:248
  488.4 84.0 %all-gather.32.cloned.1.call-start = ((), (), s32[]{:S(2)}) async-start(), calls=%async_computation.28 | async-start | bytes 1966080 | tf_op jit(solution)/shard_map/all_gather | solution.py:236
  489.2 106.8 %all-gather.30.cloned.1.call-start = ((), (), s32[]{:S(2)}) async-start(), calls=%async_computation.27 | async-start | bytes 1966080 | tf_op jit(solution)/shard_map/all_gather | solution.py:236
  559.1 78.0 %reduce-scatter.18.cloned.1.call-start = ((), (), s32[]{:S(2)}) async-start(), calls=%async_computation.22 | async-start | bytes 1966080 | tf_op jit(solution)/shard_map/reduce_scatter | solution.py:185
  595.4 61.3 %reduce-scatter.16.cloned.1.call-start = ((), (), s32[]{:S(2)}) async-start(), calls=%async_computation.21 | async-start | bytes 1966080 | tf_op jit(solution)/shard_map/reduce_scatter | solution.py:185
  619.9 77.2 %reduce-scatter.22.cloned.1.call-start = ((), (), s32[]{:S(2)}) async-start(), calls=%async_computation.24 | async-start | bytes 3932160 | tf_op jit(solution)/shard_map/reduce_scatter | solution.py:248
  627.8 109.8 %reduce-scatter.24.cloned.1.call-start = ((), (), s32[]{:S(2)}) async-start(), calls=%async_computation.25 | async-start | bytes 3932160 | tf_op jit(solution)/shard_map/reduce_scatter | solution.py:248
  635.8 271.9 %reduce-scatter.30.cloned.1.call-start = ((), (), s32[]{:S(2)}) async-start(), calls=%async_computation.31 | async-start | bytes 4866048 | tf_op jit(solution)/shard_map/reduce_scatter | solution.py:119
  773.9 220.0 %reduce-scatter.28.cloned.1.call-start = ((), (), s32[]{:S(2)}) async-start(), calls=%async_computation.30 | async-start | bytes 4866048 | tf_op jit(solution)/shard_map/reduce_scatter | solution.py:118
  786.6 328.6 %reduce-scatter.38.cloned.1.call-start = ((), (), s32[]{:S(2)}) async-start(), calls=%async_computation.35 | async-start | bytes 7077888 | tf_op jit(solution)/shard_map/reduce_scatter | solution.py:129
  797.2 439.2 %reduce-scatter.36.cloned.1.call-start = ((), (), s32[]{:S(2)}) async-start(), calls=%async_computation.34 | async-start | bytes 7077888 | tf_op jit(solution)/shard_map/reduce_scatter | solution.py:128
  807.8 549.9 %reduce-scatter.34.cloned.1.call-start = ((), (), s32[]{:S(2)}) async-start(), calls=%async_computation.33 | async-start | bytes 7077888 | tf_op jit(solution)/shard_map/reduce_scatter | solution.py:127
  818.3 680.4 %reduce-scatter.32.cloned.1.call-start = ((), (), s32[]{:S(2)}) async-start(), calls=%async_computation.32 | async-start | bytes 9732096 | tf_op jit(solution)/shard_map/reduce_scatter | solution.py:120
  827.4 813.7 %reduce-scatter.26.cloned.1.call-start = ((), (), s32[]{:S(2)}) async-start(), calls=%async_computation.29 | async-start | bytes 9732096 | tf_op jit(solution)/shard_map/reduce_scatter | solution.py:117
  (198 other events, 1265.9 us)
Sparse Core Ops, SparseCore 0:
  11.0 60.1 all-gather.13
  74.0 55.9 all-gather.15
  133.0 62.5 all-gather.17
  198.3 62.4 all-gather.19
  262.7 21.0 all-gather.27
  285.9 60.4 all-gather.25
  348.6 59.0 all-gather.23
  409.9 59.0 all-gather.21
  480.8 26.7 reduce-scatter.13
  510.2 37.9 reduce-scatter.19
  549.7 22.7 all-gather.31
  573.9 20.7 all-gather.29
  597.2 28.1 reduce-scatter.17
  628.5 28.1 reduce-scatter.15
  659.1 37.9 reduce-scatter.21
  699.6 37.9 reduce-scatter.23
  774.0 107.2 reduce-scatter.29
  888.1 105.7 reduce-scatter.27
  998.1 117.1 reduce-scatter.37
  1119.2 117.0 reduce-scatter.35
  1240.5 117.0 reduce-scatter.33
  1364.1 134.4 reduce-scatter.31
  1506.1 134.8 reduce-scatter.25
